TPU v7x, 128 devices: a whole 4x4x4 slice. The times are simulated.
128 devices in a mesh: row: 8 (over x, core), col: 16 (over y, z).
Axes of the slice: x: 4, y: 4, z: 4, core: 2. Of those that a mesh axis runs over, the one named last changes fastest.
Arguments:
- density_factor: bfloat16 [524288, 256], P(('row', 'col'))
- onsite: float32 [524288], P(('row', 'col')), may hold values from -4 to 4
- neighbour_ids: int32 [1024, 8], P(('row', 'col')), may hold values from 0 to 1023, as said below
- neighbour_count: int32 [1024], P(('row', 'col')), may hold values from 1 to 8, as said below
- coupling_type: int32 [1024, 8], P(('row', 'col')), may hold values from 0 to 3
- coupling_blocks: bfloat16 [4, 512, 512], replicated, may hold values from -0.25 to 0.25
- bath_pattern: int32 [1024], P(('row', 'col')), may hold values from 0 to 3
- bath_blocks: bfloat16 [4, 512, 512], replicated, may hold values from -0.25 to 0.25
Outputs:
- new_factor: bfloat16 [524288, 256], P(('row', 'col'))
Inputs may be any that keep to these rules, and one draw needn't show every extreme that they name: `neighbour_ids`: every neighbour of block b lies among the 128 blocks that share b's index of row, at most half of 128 blocks from b when that group is taken as a loop, and is never b itself; some block has a neighbour exactly half of 128 blocks away. Only the first neighbour_count[b] slots of block b's lists are used; some block uses all 8.
All inputs are finite; a program needn't handle non-finite values.
Results may differ from a plain program's by a relative error of at most 0.0056.
Values may be sent and summed in bfloat16 or wider, within the bound.
A program may use at most 192 MiB of HBM per device.

v0:
```python
import jax
import jax.numpy as jnp
from jax import lax
from jax.sharding import PartitionSpec as P

SWEEPS = 2
time_step = 0.25


def orthonormal_steps(gram, rank_cols):
    basis = jnp.eye(2 * rank_cols, rank_cols, dtype=jnp.float32)
    for sweep in range(SWEEPS):
        image = jnp.dot(gram, basis, precision=lax.Precision.HIGHEST)
        inner = jnp.dot(image.T, image, precision=lax.Precision.HIGHEST)
        factor = jnp.linalg.cholesky(inner)
        basis = lax.linalg.triangular_solve(
            factor, image, left_side=False, lower=True, transpose_a=True
        )
    return basis


def shards(
    density_factor,
    onsite,
    neighbour_ids,
    neighbour_count,
    coupling_type,
    coupling_blocks,
    bath_pattern,
    bath_blocks,
):
    blocks, slots = neighbour_ids.shape
    kinds = coupling_blocks.shape[0]
    block_rows = coupling_blocks.shape[1]
    rank_cols = density_factor.shape[1]
    col_count = lax.axis_size("col")
    group_blocks = col_count * blocks
    row_place = lax.axis_index("row")
    in_group = neighbour_ids - row_place * group_blocks
    slot_live = jnp.arange(slots, dtype=jnp.int32)[None, :] < neighbour_count[:, None]
    kind_match = (
        coupling_type[:, :, None] == jnp.arange(kinds, dtype=jnp.int32)[None, None, :]
    ) & slot_live[:, :, None]
    kind_float = kind_match.astype(jnp.float32)
    gathered = lax.all_gather(density_factor, "col", axis=0, tiled=True)
    hits = (
        in_group[:, :, None] == jnp.arange(group_blocks, dtype=jnp.int32)[None, None, :]
    ).astype(jnp.float32)
    mixing = jnp.einsum("bkt,bkn->btn", kind_float, hits).astype(jnp.bfloat16)
    flat_blocks = gathered.reshape(group_blocks, block_rows * rank_cols)
    summed = jnp.einsum("btn,nm->btm", mixing, flat_blocks, preferred_element_type=jnp.float32)
    summed = summed.reshape(blocks, kinds, block_rows, rank_cols).astype(jnp.bfloat16)
    coupled = jnp.einsum(
        "tij,btjr->bir", coupling_blocks, summed, preferred_element_type=jnp.float32
    )
    own_rows = density_factor.reshape(blocks, block_rows, rank_cols)
    bath_pick = bath_blocks[bath_pattern]
    bathed = jnp.einsum(
        "bij,bjr->bir", bath_pick, own_rows, preferred_element_type=jnp.float32
    ).astype(jnp.bfloat16)
    factor_wide = own_rows.astype(jnp.float32)
    energy = onsite.reshape(blocks, block_rows, 1)
    moved = (factor_wide - time_step * (energy * factor_wide + coupled)).astype(jnp.bfloat16)
    stacked = jnp.concatenate([moved, bathed], axis=2).reshape(blocks * block_rows, 2 * rank_cols)
    local_gram = lax.dot_general(
        stacked, stacked, (((0,), (0,)), ((), ())), preferred_element_type=jnp.float32
    )
    gram_sum = lax.psum(local_gram, ("row", "col"))
    rotation = orthonormal_steps(gram_sum, rank_cols).astype(jnp.bfloat16)
    return jnp.dot(stacked, rotation, preferred_element_type=jnp.float32).astype(jnp.bfloat16)


def solution(mesh):
    placed = (
        P(("row", "col"), None),
        P(("row", "col")),
        P(("row", "col"), None),
        P(("row", "col")),
        P(("row", "col"), None),
        P(),
        P(("row", "col")),
        P(),
    )
    return jax.shard_map(
        shards, mesh=mesh, in_specs=placed, out_specs=P(("row", "col"), None), check_vma=False
    )
```

profile of v0, /device:TPU:1, one launch (start us, length us, event | category | flops | bytes accessed | tf_op | source)
XLA Modules:
  0.0 618.0 jit_solution(14788270948122039171)
XLA Ops:
  6.5 0.7 all-gather.2.cloned.1.call-update
  7.3 0.7 mul.19
  8.0 3.9 copy.12
  12.0 2.9 gather_fusion
  14.9 4.2 convolution_convert_fusion.1
  19.1 190.8 %all-gather.2.cloned.1.call-done = bf16[65536,256]{1,0:T(8,128)(2,1)} async-done(((bf16[4096,256]{1,0:T(8,128)(2,1)}), bf16[65536,256]{1,0:T(8,128)(2,1)}) %all-gather.2.cloned.1.call-update) | async-done | bytes 33554448 | tf_op jit(solution)/shard_map/all_gather | solution.py:45
  210.0 33.2 %reshape.54 = bf16[128,131072]{1,0:T(8,128)(2,1)} reshape(bf16[65536,256]{1,0:T(8,128)(2,1)} %all-gather.2.cloned.1.call-done) | data formatting | bytes 67108864 | tf_op jit(solution)/shard_map/reshape | solution.py:50
  243.2 23.1 %copy.24 = bf16[16,8,512,256]{3,2,1,0:T(8,128)(2,1)} copy(bf16[16,8,512,256]{3,1,2,0:T(8,128)(2,1)} %bitcast.98) | data formatting | bytes 67108864
  266.2 36.0 %fusion = bf16[8,4,512,256]{3,1,2,0:T(4,128)(2,1)} fusion(bf16[512,256,128,1]{1,0,2,3:T(8,128)(2,1)} %bitcast.99, s32[8,8]{1,0:T(8,128)S(1)} %broadcast_subtract_fusion, s32[8,8]{1,0:T(8,128)S(1)} %copy-done.5, pred[8,8]{1,0:T(8,128)(4,1)S(1)} %iota_compare_fusion.9), kind=kOutput, calls=%fused_computation.5 | convolution fusion | flops 1073820160 | bytes 41943616 | tf_op jit(solution)/shard_map/btn,nm->btm/dot_general | solution.py:51
  302.3 13.8 %copy.20 = bf16[8,4,512,256]{2,3,1,0:T(8,128)(2,1)} copy(bf16[8,4,512,256]{3,1,2,0:T(4,128)(2,1)} %fusion) | data formatting | bytes 16777216 | tf_op jit(solution)/shard_map/btn,nm->btm/dot_general | solution.py:51
  316.1 9.6 %fusion.6 = bf16[8,512,256]{1,2,0:T(8,128)(2,1)S(1)} fusion(bf16[8,512,256]{1,2,0:T(8,128)(2,1)} %copy.12, bf16[8,4,512,256]{2,3,1,0:T(8,128)(2,1)} %copy.20, bf16[4,512,512]{2,1,0:T(8,128)(2,1)} %param.16, f32[8,512]{1,0:T(8,128)S(1)} %mul.19), kind=kOutput, calls=%fused_computation.14 | convolution fusion | flops 4301258752 | bytes 14696448 | tf_op jit(solution)/shard_map/tij,btjr->bir/dot_general | solution.py:53
  325.7 1.3 copy-done.3
  327.0 3.3 convolution_bitcast_fusion
  330.3 3.8 pad_maximum_fusion
  334.2 6.5 %copy.14 = bf16[8,512,512]{2,1,0:T(8,128)(2,1)} copy(bf16[8,512,512]{1,2,0:T(8,128)(2,1)} %pad_maximum_fusion) | data formatting | bytes 8388608 | tf_op jit(solution)/shard_map/concatenate | solution.py:64
  340.6 136.9 %all-reduce.3.cloned.1.call-done = f32[512,512]{1,0:T(8,128)} async-done(((f32[512,512]{1,0:T(8,128)}), f32[512,512]{1,0:T(8,128)}) %all-reduce.3.cloned.1.call-update) | async-done | bytes 1048592 | tf_op jit(solution)/shard_map/psum | solution.py:68
  477.5 1.9 fusion.15
  479.4 1.0 fusion.49
  480.7 11.7 %cholesky.130 = f32[128,128]{1,0:T(8,128)S(1)} custom-call(f32[128,128]{1,0:T(8,128)S(1)} %cholesky.194), custom_call_target="Cholesky" | custom-call | tf_op jit(solution)/shard_map/jit(cholesky)/cholesky | solution.py:15
  492.4 9.8 %custom-call.13 = f32[1,128,128]{1,2,0:T(8,128)S(1)} custom-call(f32[1,128,128]{2,1,0:T(8,128)S(1)} %get-tuple-element.50), custom_call_target="InvertDiagBlocksLowerTriangular" | custom-call | tf_op jit(solution)/shard_map/jit(cholesky)/cholesky | solution.py:15
  502.7 11.7 %cholesky.147 = f32[128,128]{1,0:T(8,128)S(1)} custom-call(f32[128,128]{1,0:T(8,128)S(1)} %convolution_subtract_fusion.3), custom_call_target="Cholesky" | custom-call | tf_op jit(solution)/shard_map/jit(cholesky)/cholesky | solution.py:15
  514.5 0.7 compare_reduce_fusion.2
  516.6 4.0 while.4
  516.6 0.6 fusion.71
  517.2 1.4 bitcast_dynamic-update-slice_fusion.4
  518.6 0.6 fusion.71
  519.2 1.4 bitcast_dynamic-update-slice_fusion.4
  520.6 20.1 %custom-call.14 = f32[2,128,128]{1,2,0:T(8,128)S(1)} custom-call(f32[2,128,128]{2,1,0:T(8,128)S(1)} %get-tuple-element.21), custom_call_target="InvertDiagBlocksLowerTriangular" | custom-call | tf_op jit(solution)/shard_map/triangular_solve/custom-call.0 | solution.py:16
  540.6 0.4 fusion.18
  541.1 0.6 convolution_subtract_fusion.1
  541.7 0.4 fusion.26
  542.1 1.0 fusion.11
  543.1 1.0 fusion.50
  544.3 11.7 %cholesky.164 = f32[128,128]{1,0:T(8,128)S(1)} custom-call(f32[128,128]{1,0:T(8,128)S(1)} %cholesky.197), custom_call_target="Cholesky" | custom-call | tf_op jit(solution)/shard_map/jit(cholesky)/cholesky | solution.py:15
  556.1 0.6 compare_reduce_fusion.1
  556.7 9.8 %custom-call.15 = f32[1,128,128]{1,2,0:T(8,128)S(1)} custom-call(f32[1,128,128]{2,1,0:T(8,128)S(1)} %get-tuple-element.46), custom_call_target="InvertDiagBlocksLowerTriangular" | custom-call | tf_op jit(solution)/shard_map/jit(cholesky)/cholesky | solution.py:15
  567.1 11.9 %cholesky.181 = f32[128,128]{1,0:T(8,128)S(1)} custom-call(f32[128,128]{1,0:T(8,128)S(1)} %convolution_subtract_fusion.2), custom_call_target="Cholesky" | custom-call | tf_op jit(solution)/shard_map/jit(cholesky)/cholesky | solution.py:15
  579.0 0.6 compare_reduce_fusion
  580.9 3.9 while.5
  581.0 0.6 fusion.72
  581.5 1.4 bitcast_dynamic-update-slice_fusion.5
  582.9 0.6 fusion.72
  583.5 1.4 bitcast_dynamic-update-slice_fusion.5
  584.9 19.7 %custom-call.16 = f32[2,128,128]{1,2,0:T(8,128)S(1)} custom-call(f32[2,128,128]{2,1,0:T(8,128)S(1)} %get-tuple-element.22), custom_call_target="InvertDiagBlocksLowerTriangular" | custom-call | tf_op jit(solution)/shard_map/triangular_solve/custom-call.0 | solution.py:16
  604.6 0.4 fusion.16
  605.0 0.6 convolution_subtract_fusion
  605.6 0.4 fusion.22
  606.0 4.9 convolution_convert_fusion
  (48 shorter events, 1.8 us)
Async XLA Ops:
  6.5 5.4 copy-start
  6.5 5.4 copy-start.6
  6.5 203.4 %all-gather.2.cloned.1.call-start = ((), (), s32[]{:S(2)}) async-start(), calls=%async_computation | async-start | bytes 35651584 | tf_op jit(solution)/shard_map/all_gather | solution.py:45
  7.3 470.3 %all-reduce.3.cloned.1.call-start = ((), (), s32[]{:S(2)}) async-start(), calls=%async_computation.1 | async-start | bytes 2097152 | tf_op jit(solution)/shard_map/psum | solution.py:68
  12.0 2.9 copy-start.7
  12.0 3.0 copy-start.4
  243.2 23.1 %copy-start.5 = (s32[8,8]{1,0:T(8,128)S(1)}, s32[8,8]{1,0:T(8,128)}, u32[]{:S(2)}) copy-start(s32[8,8]{1,0:T(8,128)} %param.15) | copy-start | bytes 772
  325.6 1.3 copy-start.3
  477.5 64.6 %copy-start.2 = (f32[512,512]{1,0:T(8,128)S(1)}, f32[512,512]{1,0:T(8,128)}, u32[]{:S(2)}) copy-start(f32[512,512]{1,0:T(8,128)} %all-reduce.3.cloned.1.call-done) | copy-start | bytes 3145732
  606.0 5.0 copy-start.1
Sparse Core Ops, SparseCore 0:
  9.5 200.4 all-gather.1
  330.4 147.0 all-reduce.2
where the time goes:
time: 623 us; the launch traced here: 618 us
  waiting for transfers between devices  328 us (53%)
  other arithmetic  113 us (18%)
  local copies, waits for them, and re-layouts  93.6 us (15%)
  matrix products  66.8 us (11%)
  between operations  16.5 us (3%)
    all_gather x1, waiting for transfers between devices, shards(): gathered = lax.all_gather(density_factor, 'col', axis=0, tiled=True)  191 us
    psum x1, waiting for transfers between devices, shards(): gram_sum = lax.psum(local_gram, ('row', 'col'))  137 us
    another operation x13, other arithmetic, orthonormal_steps(): factor = jnp.linalg.cholesky(inner)  68.8 us
    another operation x5, other arithmetic, orthonormal_steps(): lax.linalg.triangular_solve(factor, image, left_side=False, lower=True, t...  39.8 us
    dot_general x1, matrix products, shards(): jnp.einsum('btn,nm->btm', mixing, flat_blocks, preferred_element_type=jnp...  36 us
    reshape x1, local copies, waits for them, and re-layouts, shards(): flat_blocks = gathered.reshape(group_blocks, block_rows * rank_cols)  33.2 us
    unnamed x17, local copies, waits for them, and re-layouts  24.4 us
    dot_general x1, local copies, waits for them, and re-layouts, shards(): jnp.einsum('btn,nm->btm', mixing, flat_blocks, preferred_element_type=jnp...  13.8 us
  transfers between devices with their start and end apart: 2, of which 2 were waited for; matrix products, arithmetic and copies ran while one was open for 4% of the time, Pallas kernels for 0%

commit v1 on v0

--- a/solution.py
+++ b/solution.py
@@ -42,7 +42,9 @@
         coupling_type[:, :, None] == jnp.arange(kinds, dtype=jnp.int32)[None, None, :]
     ) & slot_live[:, :, None]
     kind_float = kind_match.astype(jnp.float32)
-    gathered = lax.all_gather(density_factor, "col", axis=0, tiled=True)
+    gathered = jnp.concatenate(
+        lax.all_to_all(jnp.stack([density_factor] * lax.axis_size("col")), "col", 0, 0), axis=0
+    )
     hits = (
         in_group[:, :, None] == jnp.arange(group_blocks, dtype=jnp.int32)[None, None, :]
     ).astype(jnp.float32)

time: 623 us -> 1070 us (1.72)
  waiting for transfers between devices: 328 us -> 752 us
  local copies, waits for them, and re-layouts: 93.6 us -> 105 us
    all_to_all x0 -> x1, waiting for transfers between devices: none -> 609 us  [shards(): lax.all_to_all(jnp.stack([density_factor] * lax.axis_size('col')), 'col',...]
    all_gather x1 -> x0, waiting for transfers between devices: 191 us -> none  [shards(): gathered = lax.all_gather(density_factor, 'col', axis=0, tiled=True)]
    another operation x0 -> x2, local copies, waits for them, and re-layouts: none -> 45.4 us  [the longest x1 33.2 us: shards(): flat_blocks = gathered.reshape(group_blocks, block_rows * rank_cols)]
    reshape x1 -> x0, local copies, waits for them, and re-layouts: 33.2 us -> none  [shards(): flat_blocks = gathered.reshape(group_blocks, block_rows * rank_cols)]
    unnamed x17 -> x19, local copies, waits for them, and re-layouts: 24.4 us -> 24.4 us
  transfers between devices with their start and end apart: 2 -> 2, of which waited for: 2 -> 2; matrix products, arithmetic and copies ran while one was open for 4% -> 2% of each run, Pallas kernels for 0% -> 0%
where the time goes in v1:
time: 1070 us; the launch traced here: 1060 us
  waiting for transfers between devices  752 us (70%)
  other arithmetic  113 us (11%)
  local copies, waits for them, and re-layouts  105 us (10%)
  matrix products  66.8 us (6%)
  between operations  16.5 us (2%)
    all_to_all x1, waiting for transfers between devices, shards(): lax.all_to_all(jnp.stack([density_factor] * lax.axis_size('col')), 'col',...  609 us
    psum x1, waiting for transfers between devices, shards(): gram_sum = lax.psum(local_gram, ('row', 'col'))  143 us
    another operation x13, other arithmetic, orthonormal_steps(): factor = jnp.linalg.cholesky(inner)  68.7 us
    another operation x5, other arithmetic, orthonormal_steps(): lax.linalg.triangular_solve(factor, image, left_side=False, lower=True, t...  39.8 us
    dot_general x1, matrix products, shards(): jnp.einsum('btn,nm->btm', mixing, flat_blocks, preferred_element_type=jnp...  36 us
    another operation x1, local copies, waits for them, and re-layouts, shards(): flat_blocks = gathered.reshape(group_blocks, block_rows * rank_cols)  33.2 us
    unnamed x19, local copies, waits for them, and re-layouts  24.4 us
  transfers between devices with their start and end apart: 2, of which 2 were waited for; matrix products, arithmetic and copies ran while one was open for 2% of the time, Pallas kernels for 0%

profile of v1, /device:TPU:1, one launch (start us, length us, event | category | flops | bytes accessed | tf_op | source)
XLA Modules:
  0.0 1061.4 jit_solution(9854354641696324071)
XLA Ops:
  6.5 12.2 %stack.2 = bf16[16,4096,256]{2,1,0:T(8,128)(2,1)} broadcast(bf16[4096,256]{1,0:T(8,128)(2,1)} %param.11), dimensions={1,2} | broadcast | bytes 35651584 | tf_op jit(solution)/shard_map/stack | solution.py:46
  18.8 8.6 all-to-all-start
  27.5 3.9 copy.12
  31.5 2.8 gather_fusion
  34.4 4.2 convolution_convert_fusion.1
  38.5 608.6 %all-to-all-done = bf16[16,4096,256]{2,1,0:T(8,128)(2,1)} async-done(((bf16[16,4096,256]{2,1,0:T(8,128)(2,1)}), bf16[16,4096,256]{2,1,0:T(8,128)(2,1)}, u32[]{:S(2)}, u32[]{:S(2)}) %all-to-all-start) | async-done | bytes 33554464 | tf_op jit(solution)/shard_map/all_to_all | solution.py:46
  647.1 33.2 %reshape_reshape.3 = bf16[128,131072]{1,0:T(8,128)(2,1)} reshape(bf16[16,4096,256]{2,1,0:T(8,128)(2,1)} %all-to-all-done) | data formatting | bytes 67108864 | tf_op jit(solution)/shard_map/reshape;reshape | solution.py:52
  680.3 23.1 %copy.24 = bf16[16,8,512,256]{3,2,1,0:T(8,128)(2,1)} copy(bf16[16,8,512,256]{3,1,2,0:T(8,128)(2,1)} %bitcast.98) | data formatting | bytes 67108864
  703.4 36.0 %fusion = bf16[8,4,512,256]{3,1,2,0:T(4,128)(2,1)} fusion(bf16[512,256,128,1]{1,0,2,3:T(8,128)(2,1)} %bitcast.99, s32[8,8]{1,0:T(8,128)S(1)} %broadcast_subtract_fusion, s32[8,8]{1,0:T(8,128)S(1)} %copy-done.6, pred[8,8]{1,0:T(8,128)(4,1)S(1)} %iota_compare_fusion.9), kind=kOutput, calls=%fused_computation.5 | convolution fusion | flops 1073820160 | bytes 41943616 | tf_op jit(solution)/shard_map/btn,nm->btm/dot_general | solution.py:53
  739.4 13.8 %copy.20 = bf16[8,4,512,256]{2,3,1,0:T(8,128)(2,1)} copy(bf16[8,4,512,256]{3,1,2,0:T(4,128)(2,1)} %fusion) | data formatting | bytes 16777216 | tf_op jit(solution)/shard_map/btn,nm->btm/dot_general | solution.py:53
  753.2 9.6 fusion.6
  762.8 1.3 copy-done.3
  764.1 3.3 convolution_bitcast_fusion
  767.5 3.8 pad_maximum_fusion
  771.3 6.5 copy.14
  777.8 143.1 %all-reduce.3.cloned.1.call-done = f32[512,512]{1,0:T(8,128)} async-done(((f32[512,512]{1,0:T(8,128)}), f32[512,512]{1,0:T(8,128)}) %all-reduce.3.cloned.1.call-update) | async-done | bytes 1048592 | tf_op jit(solution)/shard_map/psum | solution.py:70
  920.9 1.9 fusion.15
  922.9 1.0 fusion.49
  924.1 11.7 %cholesky.130 = f32[128,128]{1,0:T(8,128)S(1)} custom-call(f32[128,128]{1,0:T(8,128)S(1)} %cholesky.194), custom_call_target="Cholesky" | custom-call | tf_op jit(solution)/shard_map/jit(cholesky)/cholesky | solution.py:15
  935.8 9.8 custom-call.13
  946.2 11.7 %cholesky.147 = f32[128,128]{1,0:T(8,128)S(1)} custom-call(f32[128,128]{1,0:T(8,128)S(1)} %convolution_subtract_fusion.3), custom_call_target="Cholesky" | custom-call | tf_op jit(solution)/shard_map/jit(cholesky)/cholesky | solution.py:15
  957.9 0.7 compare_reduce_fusion.2
  960.0 4.0 while.4
  960.0 0.6 fusion.71
  960.6 1.4 bitcast_dynamic-update-slice_fusion.4
  962.0 0.6 fusion.71
  962.6 1.4 bitcast_dynamic-update-slice_fusion.4
  964.0 20.1 %custom-call.14 = f32[2,128,128]{1,2,0:T(8,128)S(1)} custom-call(f32[2,128,128]{2,1,0:T(8,128)S(1)} %get-tuple-element.21), custom_call_target="InvertDiagBlocksLowerTriangular" | custom-call | tf_op jit(solution)/shard_map/triangular_solve/custom-call.0 | solution.py:16
  984.1 0.4 fusion.18
  984.5 0.6 convolution_subtract_fusion.1
  985.1 0.4 fusion.26
  985.5 1.0 fusion.11
  986.6 1.0 fusion.50
  987.8 11.7 %cholesky.164 = f32[128,128]{1,0:T(8,128)S(1)} custom-call(f32[128,128]{1,0:T(8,128)S(1)} %cholesky.197), custom_call_target="Cholesky" | custom-call | tf_op jit(solution)/shard_map/jit(cholesky)/cholesky | solution.py:15
  999.5 9.8 custom-call.15
  1009.8 11.9 %cholesky.181 = f32[128,128]{1,0:T(8,128)S(1)} custom-call(f32[128,128]{1,0:T(8,128)S(1)} %convolution_subtract_fusion.2), custom_call_target="Cholesky" | custom-call | tf_op jit(solution)/shard_map/jit(cholesky)/cholesky | solution.py:15
  1021.7 0.6 compare_reduce_fusion
  1022.4 0.6 compare_reduce_fusion.1
  1024.4 3.9 while.5
  1024.4 0.6 fusion.72
  1025.0 1.4 bitcast_dynamic-update-slice_fusion.5
  1026.4 0.6 fusion.72
  1026.9 1.4 bitcast_dynamic-update-slice_fusion.5
  1028.3 19.7 %custom-call.16 = f32[2,128,128]{1,2,0:T(8,128)S(1)} custom-call(f32[2,128,128]{2,1,0:T(8,128)S(1)} %get-tuple-element.22), custom_call_target="InvertDiagBlocksLowerTriangular" | custom-call | tf_op jit(solution)/shard_map/triangular_solve/custom-call.0 | solution.py:16
  1048.0 0.4 fusion.16
  1048.4 0.6 convolution_subtract_fusion
  1049.0 0.4 fusion.22
  1049.4 4.9 convolution_convert_fusion
  (50 shorter events, 1.8 us)
Async XLA Ops:
  6.5 24.9 %copy-start = (bf16[4,512,512]{2,1,0:T(8,128)(2,1)S(1)}, bf16[4,512,512]{2,1,0:T(8,128)(2,1)}, u32[]{:S(2)}) copy-start(bf16[4,512,512]{2,1,0:T(8,128)(2,1)} %param.18) | copy-start | bytes 6291460
  18.8 628.4 %all-to-all-start = ((bf16[16,4096,256]{2,1,0:T(8,128)(2,1)}), bf16[16,4096,256]{2,1,0:T(8,128)(2,1)}, u32[]{:S(2)}, u32[]{:S(2)}) async-start(bf16[16,4096,256]{2,1,0:T(8,128)(2,1)} %stack.2), calls=%async_computation | async-start | bytes 67108864 | tf_op jit(solution)/shard_map/all_to_all | solution.py:46
  27.4 4.0 copy-start.4
  27.4 4.0 copy-start.7
  27.4 893.5 %all-reduce.3.cloned.1.call-start = ((), (), s32[]{:S(2)}) async-start(), calls=%async_computation.1 | async-start | bytes 2097152 | tf_op jit(solution)/shard_map/psum | solution.py:70
  31.5 2.8 copy-start.8
  31.5 2.9 copy-start.5
  680.3 23.1 %copy-start.6 = (s32[8,8]{1,0:T(8,128)S(1)}, s32[8,8]{1,0:T(8,128)}, u32[]{:S(2)}) copy-start(s32[8,8]{1,0:T(8,128)} %param.15) | copy-start | bytes 772
  762.8 1.3 copy-start.3
  920.9 64.6 %copy-start.2 = (f32[512,512]{1,0:T(8,128)S(1)}, f32[512,512]{1,0:T(8,128)}, u32[]{:S(2)}) copy-start(f32[512,512]{1,0:T(8,128)} %all-reduce.3.cloned.1.call-done) | copy-start | bytes 3145732
  1049.4 5.0 copy-start.1
Sparse Core Ops, SparseCore 0:
  767.6 153.2 all-reduce.2
